TPU v7x, 256 devices: a whole 4x4x8 slice. The times are simulated.
256 devices in a mesh: section: 8 (over z), expert: 32 (over x, y, core).
Axes of the slice: x: 4, y: 4, z: 8, core: 2. Of those that a mesh axis runs over, the one named last changes fastest.
Arguments:
- grad_out: bfloat16 [4096, 4096], P('expert', 'section'), may hold values from -6 to 6
- probs: float32 [4096, 8], P('expert'), may hold values from 0.05 to 0.4
- expert_ids: int32 [4096, 8], P('expert'), may hold values from 0 to 63, all different within a row; in each aligned block of 128 rows (0 to 127, 128 to 255, ...) at most 24 rows name the same one
- w_gate: bfloat16 [64, 1536, 4096], P('expert', 'section'), may hold values from -0.09375 to 0.09375
- w_up: bfloat16 [64, 1536, 4096], P('expert', 'section'), may hold values from -0.09375 to 0.09375
- w_down: bfloat16 [64, 1536, 4096], P('expert', 'section'), may hold values from -0.15625 to 0.15625
- saved_gate: bfloat16 [64, 1536, 768], P('expert', 'section'), may hold values from -3 to 3
- saved_up: bfloat16 [64, 1536, 768], P('expert', 'section'), may hold values from -3 to 3
Outputs:
- grad_in: bfloat16 [4096, 4096], P('expert', 'section')
- grad_probs: bfloat16 [4096, 8], P('expert')
Inputs may be any that keep to these rules, and one draw needn't show every extreme that they name: `expert_ids`: each token names 8 different experts. Within the tokens of one index of expert (aligned blocks of 128 tokens) no expert is named more than 24 times, a bound that some block reaches.
All inputs are finite; a program needn't handle non-finite values.
Results may differ from a plain program's by a relative error of at most 0.015.
Values may be sent and summed in bfloat16 or wider, within the bound.
A program may use at most 128 MiB of HBM per device.

v0:
```python
import jax
import jax.numpy as jnp
from jax import lax
from jax.sharding import PartitionSpec as P

TOPK = 8


def local(grad_out, probs, expert_ids, w_gate, w_up, w_down, saved_gate, saved_up):
    groups = lax.axis_size("expert")
    local_experts = w_gate.shape[0]
    expert_count = local_experts * groups
    slot_count = saved_gate.shape[2]
    capacity = slot_count // groups
    token_count = grad_out.shape[0]
    feature_share = grad_out.shape[1]
    picked = expert_ids.reshape(-1)
    onehot = (picked[:, None] == jnp.arange(expert_count, dtype=jnp.int32)[None, :]).astype(
        jnp.int32
    )
    before = jnp.cumsum(onehot, axis=0) - onehot
    position = jnp.sum(before * onehot, axis=1)
    slot = picked * capacity + position
    owner = jnp.arange(picked.shape[0], dtype=jnp.int32) // TOPK
    table = jnp.full((expert_count * capacity,), token_count, jnp.int32).at[slot].set(owner)
    full_rows = lax.all_gather(grad_out, "section", axis=1, tiled=True)
    padded = jnp.concatenate([full_rows, jnp.zeros((1, full_rows.shape[1]), jnp.bfloat16)], axis=0)
    outgoing = padded[table].reshape(expert_count, capacity, full_rows.shape[1])
    arrived = lax.all_to_all(outgoing, "expert", split_axis=0, concat_axis=1, tiled=True)
    hidden_grad = jnp.einsum("esd,efd->efs", arrived, w_down, preferred_element_type=jnp.float32)
    gate_act = saved_gate.astype(jnp.float32)
    up_act = saved_up.astype(jnp.float32)
    sigmoid_gate = jax.nn.sigmoid(gate_act)
    silu_gate = gate_act * sigmoid_gate
    router_part = jnp.sum(silu_gate * up_act * hidden_grad, axis=1)
    router_grad = lax.psum(router_part, "section").astype(jnp.bfloat16)
    gate_grad = (
        hidden_grad * up_act * sigmoid_gate * (1.0 + gate_act * (1.0 - sigmoid_gate))
    ).astype(jnp.bfloat16)
    up_grad = (hidden_grad * silu_gate).astype(jnp.bfloat16)
    term = jnp.einsum("efc,efs->esc", w_gate, gate_grad, preferred_element_type=jnp.float32)
    term = term + jnp.einsum("efc,efs->esc", w_up, up_grad, preferred_element_type=jnp.float32)
    shares = lax.psum_scatter(term.astype(jnp.bfloat16), "section", scatter_dimension=2, tiled=True)
    back_grad, back_router = (
        lax.all_to_all(shares, "expert", split_axis=1, concat_axis=0, tiled=True),
        lax.all_to_all(router_grad, "expert", split_axis=1, concat_axis=0, tiled=True),
    )
    rows = back_grad.reshape(expert_count * capacity, feature_share)[slot]
    weighted = (
        rows.astype(jnp.float32).reshape(token_count, TOPK, feature_share) * probs[:, :, None]
    )
    grad_in = jnp.sum(weighted, axis=1).astype(jnp.bfloat16)
    grad_probs = back_router.reshape(-1)[slot].reshape(token_count, TOPK)
    return (grad_in, grad_probs)


def solution(mesh):
    placed = (
        P("expert", "section"),
        P("expert", None),
        P("expert", None),
        P("expert", "section", None),
        P("expert", "section", None),
        P("expert", "section", None),
        P("expert", "section", None),
        P("expert", "section", None),
    )
    return jax.shard_map(
        local,
        mesh=mesh,
        in_specs=placed,
        out_specs=(P("expert", "section"), P("expert", None)),
        check_vma=False,
    )
```

profile of v0, /device:TPU:1, one launch (start us, length us, event | category | flops | bytes accessed | tf_op | source)
XLA Modules:
  0.0 454.7 jit_solution(9075502163950577890)
XLA Ops:
  7.2 0.0 copy-start
  7.2 0.0 copy-start.1
  7.2 0.0 all-gather.2.cloned.1.call-start
  7.2 0.7 all-gather.2.cloned.1.call-update
  7.9 0.0 reduce-scatter.2.cloned.1.call-start
  8.0 0.9 copy.23
  8.9 0.1 eq.29
  9.0 0.1 eq.25
  9.1 0.7 fusion.16
  9.8 30.8 %reduce-window.6 = s32[64,8,128]{2,1,0:T(8,128)S(1)} reduce-window(s32[64,8,128]{2,1,0:T(8,128)} %fusion.16, s32[]{:T(128)} %constant.30.clone.1), window={size=1x1x128 pad=0_0x0_0x127_0}, to_apply=%region_0.0 | reduce-window | flops 8323072 | bytes 524292 | tf_op jit(solution)/shard_map/reduce-window
  40.7 0.9 slice.14
  41.5 1.1 copy.25
  42.6 0.1 copy.26
  42.7 0.0 copy-done.1
  42.7 0.1 copy.22
  42.9 0.1 mul.53
  43.0 0.1 broadcast_add_fusion
  43.1 0.1 fusion.15
  43.2 4.3 scatter_custom_fusion
  47.5 0.0 all-gather.2.cloned.1.call-done
  47.6 2.4 concatenate.3
  50.0 23.4 %gather_fusion = bf16[1536,4096]{1,0:T(8,128)(2,1)} fusion(bf16[129,4096]{1,0:T(8,128)(2,1)} %concatenate.3, s32[2048]{0:T(1024)S(1)} %pad_clamp_fusion), kind=kCustom, calls=%fused_computation | custom fusion | bytes 25171968 | tf_op jit(solution)/shard_map/gather | solution.py:28
  73.4 152.6 %all_to_all.49 = bf16[64,24,4096]{2,1,0:T(8,128)(2,1)S(1)} all-to-all(bf16[64,24,4096]{2,1,0:T(8,128)(2,1)} %bitcast.40), channel_id=1, replica_groups=mesh['section'=8,'expert'=32] {'expert'}, dimensions={0} | all-to-all | bytes 25165824 | tf_op jit(solution)/shard_map/all_to_all | solution.py:29
  226.0 5.2 %copy.27 = bf16[2,32,24,4096]{3,2,1,0:T(8,128)(2,1)} copy(bf16[2,32,24,4096]{3,2,0,1:T(8,128)(2,1)S(1)} %bitcast.41) | data formatting | bytes 25165824 | tf_op jit(solution)/shard_map/all_to_all | solution.py:29
  231.1 11.1 %fusion.5 = (f32[2,768]{1,0:T(2,128)S(1)}, f32[2,192,768]{2,1,0:T(8,128)}) fusion(bf16[2,192,768]{2,1,0:T(8,128)(2,1)} %param.15, bf16[2,192,768]{2,1,0:T(8,128)(2,1)} %param.14, bf16[2,768,4096]{2,1,0:T(8,128)(2,1)} %bitcast.42, bf16[2,192,4096]{2,1,0:T(8,128)(2,1)} %param.13), kind=kOutput, calls=%fused_computation.17 | convolution fusion | flops 2418571776 | bytes 18094080 | tf_op jit(solution)/shard_map/esd,efd->efs/dot_general | solution.py:30
  242.2 0.0 copy-done
  242.2 11.8 %fusion.10 = f32[2,768,4096]{2,1,0:T(8,128)} fusion(bf16[2,192,4096]{2,1,0:T(8,128)(2,1)S(1)} %copy-done, f32[2,192,768]{2,1,0:T(8,128)} %get-tuple-element.7, bf16[2,192,768]{2,1,0:T(8,128)(2,1)} %param.15, bf16[2,192,768]{2,1,0:T(8,128)(2,1)} %param.14), kind=kOutput, calls=%fused_computation.23 | convolution fusion | flops 2419458048 | bytes 30670848 | tf_op jit(solution)/shard_map/efc,efs->esc/dot_general | solution.py:41
  254.1 16.5 %add_convert_fusion = bf16[2,768,4096]{2,1,0:T(8,128)(2,1)} fusion(f32[2,768,4096]{2,1,0:T(8,128)} %fusion.10, bf16[2,192,4096]{2,1,0:T(8,128)(2,1)} %param.12, f32[2,192,768]{2,1,0:T(8,128)} %get-tuple-element.7, bf16[2,192,768]{2,1,0:T(8,128)(2,1)} %param.14), kind=kOutput, calls=%fused_computation.4 | convolution fusion | flops 2430566400 | bytes 42663936 | tf_op jit(solution)/shard_map/efc,efs->esc/dot_general | solution.py:42
  270.5 0.0 reduce-scatter.2.cloned.1.call-update
  270.6 14.2 %psum.7 = bf16[2,768]{1,0:T(2,128)(2,1)S(1)} all-reduce(f32[2,768]{1,0:T(2,128)S(1)} %get-tuple-element.6), channel_id=1, replica_groups=mesh['section'=8,'expert'=32] {'section'}, use_global_device_ids=true, to_apply=%region_7.8 | all-reduce | flops 1536 | bytes 9216 | tf_op jit(solution)/shard_map/psum | solution.py:36
  284.8 0.1 all_to_all.43
  284.9 0.6 copy.31
  285.5 6.8 %all-to-all-start.2 = ((bf16[2,32,24]{2,0,1:T(2,128)(2,1)}), bf16[2,32,24]{2,0,1:T(2,128)(2,1)S(1)}, u32[]{:S(2)}, u32[]{:S(2)}) async-start(bf16[2,32,24]{2,0,1:T(2,128)(2,1)} %copy.31), calls=%async_computation.3 | async-start | bytes 32768 | tf_op jit(solution)/shard_map/all_to_all | solution.py:46
  292.3 108.8 %reduce-scatter.2.cloned.1.call-done = bf16[2,768,512]{2,1,0:T(8,128)(2,1)} async-done(((bf16[2,768,4096]{2,1,0:T(8,128)(2,1)}), bf16[2,768,512]{2,1,0:T(8,128)(2,1)}) %reduce-scatter.2.cloned.1.call-update) | async-done | bytes 1572880 | tf_op jit(solution)/shard_map/reduce_scatter | solution.py:43
  401.1 4.2 copy.28
  405.3 0.0 copy-start.2
  405.3 0.0 all-to-all-done.2
  405.3 7.6 %all-to-all-start.1 = ((bf16[2,768,512]{2,0,1:T(2,128)(2,1)}), bf16[2,768,512]{2,0,1:T(2,128)(2,1)}, u32[]{:S(2)}, u32[]{:S(2)}) async-start(bf16[2,768,512]{2,0,1:T(2,128)(2,1)} %copy.28), calls=%async_computation.2 | async-start | bytes 3145728 | tf_op jit(solution)/shard_map/all_to_all | solution.py:45
  412.9 0.0 copy-done.2
  412.9 0.1 copy.30
  413.0 0.1 reshape.75
  413.1 6.8 %gather_fusion.2 = bf16[1024]{0:T(1024)(128)(2,1)S(1)} fusion(bf16[1536]{0:T(1024)(128)(2,1)S(1)} %reshape.75, s32[1024]{0:T(1024)S(1)} %broadcast_clamp_fusion), kind=kCustom, calls=%fused_computation.2 | custom fusion | bytes 8192 | tf_op jit(solution)/shard_map/gather | solution.py:53
  419.9 0.1 reshape.76
  420.0 0.7 copy.32
  420.7 14.9 %all-to-all-done.1 = bf16[2,768,512]{2,0,1:T(2,128)(2,1)} async-done(((bf16[2,768,512]{2,0,1:T(2,128)(2,1)}), bf16[2,768,512]{2,0,1:T(2,128)(2,1)}, u32[]{:S(2)}, u32[]{:S(2)}) %all-to-all-start.1) | async-done | bytes 1572896 | tf_op jit(solution)/shard_map/all_to_all | solution.py:45
  435.6 2.9 copy.29
  438.5 6.7 %gather_fusion.1 = bf16[1024,512]{1,0:T(8,128)(2,1)} fusion(bf16[1536,512]{1,0:T(8,128)(2,1)} %bitcast.39, s32[1024]{0:T(1024)S(1)} %broadcast_clamp_fusion), kind=kCustom, calls=%fused_computation.1 | custom fusion | bytes 2101248 | tf_op jit(solution)/shard_map/gather | solution.py:48
  445.2 2.6 fusion
  (8 shorter events, 0.1 us)
Async XLA Ops:
  7.2 235.1 %copy-start = (bf16[2,192,4096]{2,1,0:T(8,128)(2,1)S(1)}, bf16[2,192,4096]{2,1,0:T(8,128)(2,1)}, u32[]{:S(2)}) copy-start(bf16[2,192,4096]{2,1,0:T(8,128)(2,1)} %param.11) | copy-start | bytes 9437188
  7.2 35.6 %copy-start.1 = (s32[128,8]{0,1:T(8,128)S(1)}, s32[128,8]{0,1:T(8,128)}, u32[]{:S(2)}) copy-start(s32[128,8]{0,1:T(8,128)} %param.10) | copy-start | bytes 12292
  7.2 40.4 %all-gather.2.cloned.1.call-start = ((), (), s32[]{:S(2)}) async-start(), calls=%async_computation.4 | async-start | bytes 1179648 | tf_op jit(solution)/shard_map/all_gather | solution.py:26
  7.9 393.2 %reduce-scatter.2.cloned.1.call-start = ((), (), s32[]{:S(2)}) async-start(), calls=%async_computation.5 | async-start | bytes 14155776 | tf_op jit(solution)/shard_map/reduce_scatter | solution.py:43
  285.5 119.8 %all-to-all-start.2 = ((bf16[2,32,24]{2,0,1:T(2,128)(2,1)}), bf16[2,32,24]{2,0,1:T(2,128)(2,1)S(1)}, u32[]{:S(2)}, u32[]{:S(2)}) async-start(bf16[2,32,24]{2,0,1:T(2,128)(2,1)} %copy.31), calls=%async_computation.3 | async-start | bytes 32768 | tf_op jit(solution)/shard_map/all_to_all | solution.py:46
  405.3 7.6 %copy-start.2 = (f32[128,8]{0,1:T(8,128)S(1)}, f32[128,8]{0,1:T(8,128)}, u32[]{:S(2)}) copy-start(f32[128,8]{0,1:T(8,128)} %param.9) | copy-start | bytes 12292
  405.3 30.3 %all-to-all-start.1 = ((bf16[2,768,512]{2,0,1:T(2,128)(2,1)}), bf16[2,768,512]{2,0,1:T(2,128)(2,1)}, u32[]{:S(2)}, u32[]{:S(2)}) async-start(bf16[2,768,512]{2,0,1:T(2,128)(2,1)} %copy.28), calls=%async_computation.2 | async-start | bytes 3145728 | tf_op jit(solution)/shard_map/all_to_all | solution.py:45
Sparse Core Ops, SparseCore 0:
  9.8 37.5 all-gather.1
  270.7 130.3 reduce-scatter.1
where the time goes:
time: 457 us; the launch traced here: 455 us
  blocking collectives  167 us (37%)
  waiting for transfers between devices  124 us (27%)
  local copies, waits for them, and re-layouts  60.9 us (13%)
  matrix products  39.4 us (9%)
  other arithmetic  34.4 us (8%)
  starting transfers between devices  14.5 us (3%)
  between operations  14.2 us (3%)
    all_to_all x1, blocking collectives, local(): lax.all_to_all(outgoing, 'expert', split_axis=0, concat_axis=1, tiled=True)  153 us
    reduce_scatter x1, waiting for transfers between devices, local(): lax.psum_scatter(term.astype(jnp.bfloat16), 'section', scatter_dimension=...  109 us
    another operation x3, other arithmetic  31 us
    gather x1, local copies, waits for them, and re-layouts, local(): outgoing = padded[table].reshape(expert_count, capacity, full_rows.shape[1])  23.4 us
    dot_general x1, matrix products, local(): jnp.einsum('efc,efs->esc', w_up, up_grad, preferred_element_type=jnp.floa...  16.5 us
    all_to_all x1, waiting for transfers between devices, local(): lax.all_to_all(shares, 'expert', split_axis=1, concat_axis=0, tiled=True)  14.9 us
    psum x1, blocking collectives, local(): router_grad = lax.psum(router_part, 'section').astype(jnp.bfloat16)  14.2 us
    dot_general x1, matrix products, local(): jnp.einsum('efc,efs->esc', w_gate, gate_grad, preferred_element_type=jnp....  11.8 us
  transfers between devices with their start and end apart: 4, of which 2 were waited for; matrix products, arithmetic and copies ran while one was open for 11% of the time, Pallas kernels for 0%

commit v1 on v0

--- a/solution.py
+++ b/solution.py
@@ -33,7 +33,7 @@
     sigmoid_gate = jax.nn.sigmoid(gate_act)
     silu_gate = gate_act * sigmoid_gate
     router_part = jnp.sum(silu_gate * up_act * hidden_grad, axis=1)
-    router_grad = lax.psum(router_part, "section").astype(jnp.bfloat16)
+    router_grad = jnp.sum(lax.all_gather(router_part, "section"), axis=0).astype(jnp.bfloat16)
     gate_grad = (
         hidden_grad * up_act * sigmoid_gate * (1.0 + gate_act * (1.0 - sigmoid_gate))
     ).astype(jnp.bfloat16)

time: 457 us -> 457 us (level)
  waiting for transfers between devices: 124 us -> 116 us
  blocking collectives: 167 us -> 173 us
    all_gather x0 -> x1, blocking collectives: none -> 20.6 us  [local(): lax.all_gather(router_part, 'section')]
    psum x1 -> x0, blocking collectives: 14.2 us -> none  [local(): router_grad = lax.psum(router_part, 'section').astype(jnp.bfloat16)]
    reduce_scatter x1, waiting for transfers between devices: 109 us -> 101 us  [local(): lax.psum_scatter(term.astype(jnp.bfloat16), 'section', scatter_dimension=...]
where the time goes in v1:
time: 457 us; the launch traced here: 455 us
  blocking collectives  173 us (38%)
  waiting for transfers between devices  116 us (25%)
  local copies, waits for them, and re-layouts  60.9 us (13%)
  matrix products  39.4 us (9%)
  other arithmetic  34.5 us (8%)
  starting transfers between devices  16.5 us (4%)
  between operations  14.2 us (3%)
    all_to_all x1, blocking collectives, local(): lax.all_to_all(outgoing, 'expert', split_axis=0, concat_axis=1, tiled=True)  153 us
    reduce_scatter x1, waiting for transfers between devices, local(): lax.psum_scatter(term.astype(jnp.bfloat16), 'section', scatter_dimension=...  101 us
    another operation x3, other arithmetic  31 us
    gather x1, local copies, waits for them, and re-layouts, local(): outgoing = padded[table].reshape(expert_count, capacity, full_rows.shape[1])  23.4 us
    all_gather x1, blocking collectives, local(): lax.all_gather(router_part, 'section')  20.6 us
    dot_general x1, matrix products, local(): jnp.einsum('efc,efs->esc', w_up, up_grad, preferred_element_type=jnp.floa...  16.5 us
    all_to_all x1, waiting for transfers between devices, local(): lax.all_to_all(shares, 'expert', split_axis=1, concat_axis=0, tiled=True)  14.9 us
    dot_general x1, matrix products, local(): jnp.einsum('efc,efs->esc', w_gate, gate_grad, preferred_element_type=jnp....  11.8 us
  transfers between devices with their start and end apart: 4, of which 2 were waited for; matrix products, arithmetic and copies ran while one was open for 11% of the time, Pallas kernels for 0%

profile of v1, /device:TPU:1, one launch (start us, length us, event | category | flops | bytes accessed | tf_op | source)
XLA Modules:
  0.0 454.8 jit_solution(803238514626940196)
XLA Ops:
  7.2 0.0 copy-start
  7.2 0.0 copy-start.1
  7.2 0.0 all-gather.4.cloned.1.call-start
  7.2 0.7 all-gather.4.cloned.1.call-update
  7.9 0.0 reduce-scatter.2.cloned.1.call-start
  8.0 0.9 copy.23
  8.9 0.1 eq.29
  9.0 0.1 eq.25
  9.1 0.7 fusion.16
  9.8 30.8 %reduce-window.6 = s32[64,8,128]{2,1,0:T(8,128)S(1)} reduce-window(s32[64,8,128]{2,1,0:T(8,128)} %fusion.16, s32[]{:T(128)} %constant.30.clone.1), window={size=1x1x128 pad=0_0x0_0x127_0}, to_apply=%region_0.0 | reduce-window | flops 8323072 | bytes 524292 | tf_op jit(solution)/shard_map/reduce-window
  40.7 0.9 slice.14
  41.5 1.1 copy.25
  42.6 0.1 copy.26
  42.7 0.0 copy-done.1
  42.7 0.1 copy.22
  42.9 0.1 mul.53
  43.0 0.1 broadcast_add_fusion
  43.1 0.1 fusion.15
  43.2 4.3 scatter_custom_fusion
  47.5 0.0 all-gather.4.cloned.1.call-done
  47.6 2.4 concatenate.3
  50.0 23.4 %gather_fusion = bf16[1536,4096]{1,0:T(8,128)(2,1)} fusion(bf16[129,4096]{1,0:T(8,128)(2,1)} %concatenate.3, s32[2048]{0:T(1024)S(1)} %pad_clamp_fusion), kind=kCustom, calls=%fused_computation | custom fusion | bytes 25171968 | tf_op jit(solution)/shard_map/gather | solution.py:28
  73.4 152.6 %all_to_all.46 = bf16[64,24,4096]{2,1,0:T(8,128)(2,1)S(1)} all-to-all(bf16[64,24,4096]{2,1,0:T(8,128)(2,1)} %bitcast.41), channel_id=1, replica_groups=mesh['section'=8,'expert'=32] {'expert'}, dimensions={0} | all-to-all | bytes 25165824 | tf_op jit(solution)/shard_map/all_to_all | solution.py:29
  226.0 5.2 %copy.27 = bf16[2,32,24,4096]{3,2,1,0:T(8,128)(2,1)} copy(bf16[2,32,24,4096]{3,2,0,1:T(8,128)(2,1)S(1)} %bitcast.42) | data formatting | bytes 25165824 | tf_op jit(solution)/shard_map/all_to_all | solution.py:29
  231.1 11.1 %fusion.5 = (f32[2,768]{1,0:T(2,128)S(1)}, f32[2,192,768]{2,1,0:T(8,128)}) fusion(bf16[2,192,768]{2,1,0:T(8,128)(2,1)} %param.15, bf16[2,192,768]{2,1,0:T(8,128)(2,1)} %param.14, bf16[2,768,4096]{2,1,0:T(8,128)(2,1)} %bitcast.43, bf16[2,192,4096]{2,1,0:T(8,128)(2,1)} %param.13), kind=kOutput, calls=%fused_computation.17 | convolution fusion | flops 2418571776 | bytes 18094080 | tf_op jit(solution)/shard_map/esd,efd->efs/dot_general | solution.py:30
  242.2 0.0 copy-done
  242.2 11.8 %fusion.10 = f32[2,768,4096]{2,1,0:T(8,128)} fusion(bf16[2,192,4096]{2,1,0:T(8,128)(2,1)S(1)} %copy-done, f32[2,192,768]{2,1,0:T(8,128)} %get-tuple-element.7, bf16[2,192,768]{2,1,0:T(8,128)(2,1)} %param.15, bf16[2,192,768]{2,1,0:T(8,128)(2,1)} %param.14), kind=kOutput, calls=%fused_computation.23 | convolution fusion | flops 2419458048 | bytes 30670848 | tf_op jit(solution)/shard_map/efc,efs->esc/dot_general | solution.py:41
  254.1 16.5 %add_convert_fusion = bf16[2,768,4096]{2,1,0:T(8,128)(2,1)} fusion(f32[2,768,4096]{2,1,0:T(8,128)} %fusion.10, bf16[2,192,4096]{2,1,0:T(8,128)(2,1)} %param.12, f32[2,192,768]{2,1,0:T(8,128)} %get-tuple-element.7, bf16[2,192,768]{2,1,0:T(8,128)(2,1)} %param.14), kind=kOutput, calls=%fused_computation.4 | convolution fusion | flops 2430566400 | bytes 42663936 | tf_op jit(solution)/shard_map/efc,efs->esc/dot_general | solution.py:42
  270.5 0.0 reduce-scatter.2.cloned.1.call-update
  270.6 20.6 %all-gather.1 = f32[8,2,768]{2,1,0:T(2,128)S(1)} all-gather(f32[1,2,768]{2,1,0:T(2,128)S(1)} %bitcast.50), channel_id=2, replica_groups=mesh['section'=8,'expert'=32] {'section'}, dimensions={0}, use_global_device_ids=true | all-gather | bytes 55296 | tf_op jit(solution)/shard_map/all_gather | solution.py:36
  291.2 0.1 convert_element_type.50
  291.3 0.6 copy.31
  291.9 8.7 %all-to-all-start.2 = ((bf16[2,32,24]{2,0,1:T(2,128)(2,1)}), bf16[2,32,24]{2,0,1:T(2,128)(2,1)S(1)}, u32[]{:S(2)}, u32[]{:S(2)}) async-start(bf16[2,32,24]{2,0,1:T(2,128)(2,1)} %copy.31), calls=%async_computation.3 | async-start | bytes 32768 | tf_op jit(solution)/shard_map/all_to_all | solution.py:46
  300.7 100.6 %reduce-scatter.2.cloned.1.call-done = bf16[2,768,512]{2,1,0:T(8,128)(2,1)} async-done(((bf16[2,768,4096]{2,1,0:T(8,128)(2,1)}), bf16[2,768,512]{2,1,0:T(8,128)(2,1)}) %reduce-scatter.2.cloned.1.call-update) | async-done | bytes 1572880 | tf_op jit(solution)/shard_map/reduce_scatter | solution.py:43
  401.2 4.2 copy.28
  405.4 0.0 copy-start.2
  405.4 0.0 all-to-all-done.2
  405.4 7.6 %all-to-all-start.1 = ((bf16[2,768,512]{2,0,1:T(2,128)(2,1)}), bf16[2,768,512]{2,0,1:T(2,128)(2,1)}, u32[]{:S(2)}, u32[]{:S(2)}) async-start(bf16[2,768,512]{2,0,1:T(2,128)(2,1)} %copy.28), calls=%async_computation.2 | async-start | bytes 3145728 | tf_op jit(solution)/shard_map/all_to_all | solution.py:45
  413.1 0.0 copy-done.2
  413.1 0.1 copy.30
  413.2 0.1 reshape.77
  413.3 6.8 %gather_fusion.2 = bf16[1024]{0:T(1024)(128)(2,1)S(1)} fusion(bf16[1536]{0:T(1024)(128)(2,1)S(1)} %reshape.77, s32[1024]{0:T(1024)S(1)} %broadcast_clamp_fusion), kind=kCustom, calls=%fused_computation.2 | custom fusion | bytes 8192 | tf_op jit(solution)/shard_map/gather | solution.py:53
  420.1 0.1 reshape.78
  420.2 0.7 copy.32
  420.9 14.9 %all-to-all-done.1 = bf16[2,768,512]{2,0,1:T(2,128)(2,1)} async-done(((bf16[2,768,512]{2,0,1:T(2,128)(2,1)}), bf16[2,768,512]{2,0,1:T(2,128)(2,1)}, u32[]{:S(2)}, u32[]{:S(2)}) %all-to-all-start.1) | async-done | bytes 1572896 | tf_op jit(solution)/shard_map/all_to_all | solution.py:45
  435.8 2.9 copy.29
  438.7 6.7 %gather_fusion.1 = bf16[1024,512]{1,0:T(8,128)(2,1)} fusion(bf16[1536,512]{1,0:T(8,128)(2,1)} %bitcast.40, s32[1024]{0:T(1024)S(1)} %broadcast_clamp_fusion), kind=kCustom, calls=%fused_computation.1 | custom fusion | bytes 2101248 | tf_op jit(solution)/shard_map/gather | solution.py:48
  445.4 2.6 fusion
  (9 shorter events, 0.1 us)
Async XLA Ops:
  7.2 235.1 %copy-start = (bf16[2,192,4096]{2,1,0:T(8,128)(2,1)S(1)}, bf16[2,192,4096]{2,1,0:T(8,128)(2,1)}, u32[]{:S(2)}) copy-start(bf16[2,192,4096]{2,1,0:T(8,128)(2,1)} %param.11) | copy-start | bytes 9437188
  7.2 35.6 %copy-start.1 = (s32[128,8]{0,1:T(8,128)S(1)}, s32[128,8]{0,1:T(8,128)}, u32[]{:S(2)}) copy-start(s32[128,8]{0,1:T(8,128)} %param.10) | copy-start | bytes 12292
  7.2 40.4 %all-gather.4.cloned.1.call-start = ((), (), s32[]{:S(2)}) async-start(), calls=%async_computation.4 | async-start | bytes 1179648 | tf_op jit(solution)/shard_map/all_gather | solution.py:26
  7.9 393.3 %reduce-scatter.2.cloned.1.call-start = ((), (), s32[]{:S(2)}) async-start(), calls=%async_computation.5 | async-start | bytes 14155776 | tf_op jit(solution)/shard_map/reduce_scatter | solution.py:43
  291.9 113.5 %all-to-all-start.2 = ((bf16[2,32,24]{2,0,1:T(2,128)(2,1)}), bf16[2,32,24]{2,0,1:T(2,128)(2,1)S(1)}, u32[]{:S(2)}, u32[]{:S(2)}) async-start(bf16[2,32,24]{2,0,1:T(2,128)(2,1)} %copy.31), calls=%async_computation.3 | async-start | bytes 32768 | tf_op jit(solution)/shard_map/all_to_all | solution.py:46
  405.4 7.7 %copy-start.2 = (f32[128,8]{0,1:T(8,128)S(1)}, f32[128,8]{0,1:T(8,128)}, u32[]{:S(2)}) copy-start(f32[128,8]{0,1:T(8,128)} %param.9) | copy-start | bytes 12292
  405.4 30.4 %all-to-all-start.1 = ((bf16[2,768,512]{2,0,1:T(2,128)(2,1)}), bf16[2,768,512]{2,0,1:T(2,128)(2,1)}, u32[]{:S(2)}, u32[]{:S(2)}) async-start(bf16[2,768,512]{2,0,1:T(2,128)(2,1)} %copy.28), calls=%async_computation.2 | async-start | bytes 3145728 | tf_op jit(solution)/shard_map/all_to_all | solution.py:45
Sparse Core Ops, SparseCore 0:
  9.8 37.5 all-gather.3
  270.7 130.5 reduce-scatter.1
